TPU v7x, 128 devices: a whole 4x4x4 slice. The times are simulated.
128 devices in a mesh: section: 8 (over x, core), tp: 16 (over z, y).
Axes of the slice: x: 4, y: 4, z: 4, core: 2. Of those that a mesh axis runs over, the one named last changes fastest.
Arguments:
- layer_inputs: bfloat16 [16, 512, 4096], P('section', None, 'tp'), may hold values from -6 to 6
- weights: bfloat16 [16, 4096, 4096], P('section', 'tp'), may hold values from -0.046875 to 0.046875
- input_basis: bfloat16 [16, 4096, 64], P('section', 'tp'), may hold values from -0.09375 to 0.09375
- output_basis: bfloat16 [16, 4096, 32], P('section', 'tp'), may hold values from -0.09375 to 0.09375
- queries: bfloat16 [16, 512, 2048], P('section', 'tp'), may hold values from -0.00390625 to 0.00390625
- top_cotangent: bfloat16 [512, 4096], replicated, may hold values from -6 to 6
- sequence_example: int32 [4], replicated, may hold values from 0 to 1
Outputs:
- scores: float32 [2, 512], P(None, 'tp')
All inputs are finite; a program needn't handle non-finite values.
Results may differ from a plain program's by a relative error of at most 0.0094.
Values may be sent and summed in bfloat16 or wider, within the bound.
No kernel may reach another device: no remote copies, remote signals or barrier semaphores. Data moves between devices by JAX's collectives and lax.ppermute only.
A program may use at most 64 MiB of HBM per device.

v0:
```python
import jax
import jax.numpy as jnp
from jax import lax
from jax.sharding import PartitionSpec as P

SEQLEN = 128
SEQ_MB = 1
MB = 4
EXAMPLES = 2


def from_behind(value, axis, by):
    size = lax.axis_size(axis)
    pairs = [(i, i + by) for i in range(size) if 0 <= i + by < size]
    return lax.ppermute(value, axis, pairs)


def silu_parts(values):
    floats = values.astype(jnp.float32)
    logistic = jax.nn.sigmoid(floats)
    return ((floats * logistic).astype(jnp.bfloat16), logistic * (1.0 + floats * (1.0 - logistic)))


def contract_columns(portion, matrix):
    return lax.dot_general(
        portion, matrix, (((1,), (1,)), ((), ())), preferred_element_type=jnp.float32
    )


def outer_rows(out_feats, in_feats):
    joined = out_feats[:, :, :, None] * in_feats[:, :, None, :]
    return joined.reshape(joined.shape[0], joined.shape[1], -1)


def shards(
    layer_inputs, weights, input_basis, output_basis, queries, top_cotangent, sequence_example
):
    section_count = lax.axis_size("section")
    section_rank = lax.axis_index("section")
    tp_rank = lax.axis_index("tp")
    width_local = layer_inputs.shape[2]
    width_full = weights.shape[2]
    total_tokens = layer_inputs.shape[1]
    block_rows = SEQ_MB * SEQLEN
    activated, slopes = silu_parts(layer_inputs)
    partial_in = jnp.einsum(
        "ltd,ldr->tlr", activated, input_basis, preferred_element_type=jnp.float32
    )
    in_feats = lax.psum(partial_in.reshape(total_tokens, -1), "tp").reshape(partial_in.shape)
    example_index = jnp.arange(EXAMPLES, dtype=jnp.int32)
    is_top = section_rank == section_count - 1

    def fold_lower(portion):
        return contract_columns(portion, weights[0])

    def tick(tick_index, state):
        outgoing, grads, stored = state
        micro_index = tick_index - (section_count - 1 - section_rank)
        valid = (micro_index >= 0) & (micro_index < MB)
        micro_clip = jnp.clip(micro_index, 0, MB - 1)
        first_row = micro_clip * block_rows
        slope_block = lax.dynamic_slice_in_dim(slopes, first_row, block_rows, 1)
        received = from_behind(outgoing, "section", -1)
        top_block = lax.dynamic_slice_in_dim(top_cotangent, first_row, block_rows, 0)
        upper_full = jnp.where(is_top, top_block, received)
        upper_own = lax.dynamic_slice_in_dim(upper_full, tp_rank * width_local, width_local, 1)
        upper_branch = lax.dot_general(
            upper_full, weights[1], (((1,), (1,)), ((), ())), preferred_element_type=jnp.float32
        )
        middle_own = (upper_own.astype(jnp.float32) + slope_block[1] * upper_branch).astype(
            jnp.bfloat16
        )
        lower_branch = fold_lower(lax.all_gather(middle_own, "tp", axis=1, tiled=True))
        lower_own = (middle_own.astype(jnp.float32) + slope_block[0] * lower_branch).astype(
            jnp.bfloat16
        )
        new_outgoing = lax.all_gather(lower_own, "tp", axis=1, tiled=True)
        cotangents = jnp.stack([middle_own, upper_own], 0)
        partial_out = jnp.einsum(
            "lrd,ldk->rlk", cotangents, output_basis, preferred_element_type=jnp.float32
        )
        out_feats = lax.psum(partial_out.reshape(block_rows, -1), "tp").reshape(partial_out.shape)
        in_block = lax.dynamic_slice_in_dim(in_feats, first_row, block_rows, 0)
        block_examples = jnp.repeat(
            lax.dynamic_slice_in_dim(sequence_example, micro_clip * SEQ_MB, SEQ_MB, 0), SEQLEN
        )
        selector = (example_index[:, None] == block_examples[None, :]).astype(
            jnp.float32
        ) * valid.astype(jnp.float32)
        grads = grads + jnp.einsum(
            "er,rlk->lek",
            selector,
            outer_rows(out_feats, in_block),
            precision=lax.Precision.HIGHEST,
        )
        return (new_outgoing, grads, stored)

    outgoing_init = jnp.zeros((block_rows, width_full), jnp.bfloat16)
    grads_init = jnp.zeros((2, EXAMPLES, queries.shape[2]), jnp.float32)
    stored_init = jnp.zeros((1,), jnp.bfloat16)
    final_out, grads, stored = lax.fori_loop(
        0, MB + section_count - 1, tick, (outgoing_init, grads_init, stored_init)
    )
    layer_scores = jnp.einsum(
        "lek,lqk->eq", grads, queries.astype(jnp.float32), precision=lax.Precision.HIGHEST
    )
    return lax.psum(layer_scores, "section")


def solution(mesh):
    placed = (
        P("section", None, "tp"),
        P("section", "tp", None),
        P("section", "tp", None),
        P("section", "tp", None),
        P("section", "tp", None),
        P(),
        P(),
    )
    return jax.shard_map(
        shards, mesh=mesh, in_specs=placed, out_specs=P(None, "tp"), check_vma=False
    )
```

profile of v0, /device:TPU:1, one launch (start us, length us, event | category | flops | bytes accessed | tf_op | source)
XLA Modules:
  0.0 1662.4 jit_solution(13824720775074881913)
XLA Ops:
  9.2 87.7 %all-reduce.2.cloned.1.call-done = f32[512,2,64]{0,2,1:T(8,128)} async-done(((f32[512,2,64]{0,2,1:T(8,128)}), f32[512,2,64]{0,2,1:T(8,128)}) %all-reduce.2.cloned.1.call-update) | async-done | bytes 262160 | tf_op jit(solution)/shard_map/psum | solution.py:49
  98.0 1529.4 %while.18 = (s32[]{:T(128)}, bf16[128,4096]{1,0:T(8,128)(2,1)}, f32[2,2,2048]{2,1,0:T(2,128)S(1)}, pred[]{:T(512)}, s32[]{:T(128)}, /*index=5*/bf16[512,4096]{1,...) while((s32[]{:T(128)}, bf16[128,4096]{1,0:T(8,128)(2,1)}, ...), condition=%wide.region_3.4_spmd.clone, body=%wide.region_1.3_spmd.clone.sunk | while | flops 555048960 | bytes 25986044 | solution.py:101
  98.0 3.9 collective-permute-start
  101.9 13.7 collective-permute-done
  120.3 40.6 %all-gather.3.cloned.1.call-done = bf16[128,4096]{1,0:T(8,128)(2,1)} async-done(((bf16[128,256]{1,0:T(8,128)(2,1)}), bf16[128,4096]{1,0:T(8,128)(2,1)}) %all-gather.3.cloned.1.call-update) | async-done | bytes 1048592 | tf_op jit(solution)/shard_map/while/body/eval_jaxpr/all_gather | solution.py:73
  160.9 3.3 add_convert_fusion.5
  166.6 58.4 %psum.31 = f32[128,2,32]{0,2,1:T(8,128)S(1)} all-reduce(f32[128,2,32]{0,2,1:T(8,128)S(1)} %convolution_bitcast_fusion.5), channel_id=1, replica_groups=mesh['section'=8,'tp'=16] {'tp'}, use_global_device_ids=true, to_apply=%region_2.2 | all-reduce | flops 8192 | bytes 65536 | tf_op jit(solution)/shard_map/while/body/eval_jaxpr/psum | solution.py:82
  227.2 17.7 %collective-permute-start = (bf16[128,4096]{1,0:T(8,128)(2,1)}, bf16[128,4096]{1,0:T(8,128)(2,1)S(1)}, u32[]{:S(2)}, u32[]{:S(2)}) collective-permute-start(bf16[128,4096]{1,0:T(8,128)(2,1)} %get-tuple-element.465), channel_id=1, source_target_pairs={{16,0},{32,16},{48,32},{64,48},{80,64},{96,80},{112,96},{17,1},{33... | collective-permute-start | bytes 3145736 | tf_op jit(solution)/shard_map/while/body/eval_jaxpr/ppermute | solution.py:15
  244.9 13.7 collective-permute-done
  263.3 37.6 %all-gather.3.cloned.1.call-done = bf16[128,4096]{1,0:T(8,128)(2,1)} async-done(((bf16[128,256]{1,0:T(8,128)(2,1)}), bf16[128,4096]{1,0:T(8,128)(2,1)}) %all-gather.3.cloned.1.call-update) | async-done | bytes 1048592 | tf_op jit(solution)/shard_map/while/body/eval_jaxpr/all_gather | solution.py:73
  306.6 58.4 %psum.31 = f32[128,2,32]{0,2,1:T(8,128)S(1)} all-reduce(f32[128,2,32]{0,2,1:T(8,128)S(1)} %convolution_bitcast_fusion.5), channel_id=1, replica_groups=mesh['section'=8,'tp'=16] {'tp'}, use_global_device_ids=true, to_apply=%region_2.2 | all-reduce | flops 8192 | bytes 65536 | tf_op jit(solution)/shard_map/while/body/eval_jaxpr/psum | solution.py:82
  367.3 17.7 %collective-permute-start = (bf16[128,4096]{1,0:T(8,128)(2,1)}, bf16[128,4096]{1,0:T(8,128)(2,1)S(1)}, u32[]{:S(2)}, u32[]{:S(2)}) collective-permute-start(bf16[128,4096]{1,0:T(8,128)(2,1)} %get-tuple-element.465), channel_id=1, source_target_pairs={{16,0},{32,16},{48,32},{64,48},{80,64},{96,80},{112,96},{17,1},{33... | collective-permute-start | bytes 3145736 | tf_op jit(solution)/shard_map/while/body/eval_jaxpr/ppermute | solution.py:15
  385.0 13.7 collective-permute-done
  403.3 37.6 %all-gather.3.cloned.1.call-done = bf16[128,4096]{1,0:T(8,128)(2,1)} async-done(((bf16[128,256]{1,0:T(8,128)(2,1)}), bf16[128,4096]{1,0:T(8,128)(2,1)}) %all-gather.3.cloned.1.call-update) | async-done | bytes 1048592 | tf_op jit(solution)/shard_map/while/body/eval_jaxpr/all_gather | solution.py:73
  446.6 58.4 %psum.31 = f32[128,2,32]{0,2,1:T(8,128)S(1)} all-reduce(f32[128,2,32]{0,2,1:T(8,128)S(1)} %convolution_bitcast_fusion.5), channel_id=1, replica_groups=mesh['section'=8,'tp'=16] {'tp'}, use_global_device_ids=true, to_apply=%region_2.2 | all-reduce | flops 8192 | bytes 65536 | tf_op jit(solution)/shard_map/while/body/eval_jaxpr/psum | solution.py:82
  507.3 17.7 %collective-permute-start = (bf16[128,4096]{1,0:T(8,128)(2,1)}, bf16[128,4096]{1,0:T(8,128)(2,1)S(1)}, u32[]{:S(2)}, u32[]{:S(2)}) collective-permute-start(bf16[128,4096]{1,0:T(8,128)(2,1)} %get-tuple-element.465), channel_id=1, source_target_pairs={{16,0},{32,16},{48,32},{64,48},{80,64},{96,80},{112,96},{17,1},{33... | collective-permute-start | bytes 3145736 | tf_op jit(solution)/shard_map/while/body/eval_jaxpr/ppermute | solution.py:15
  525.0 13.7 collective-permute-done
  543.4 37.6 %all-gather.3.cloned.1.call-done = bf16[128,4096]{1,0:T(8,128)(2,1)} async-done(((bf16[128,256]{1,0:T(8,128)(2,1)}), bf16[128,4096]{1,0:T(8,128)(2,1)}) %all-gather.3.cloned.1.call-update) | async-done | bytes 1048592 | tf_op jit(solution)/shard_map/while/body/eval_jaxpr/all_gather | solution.py:73
  586.7 58.4 %psum.31 = f32[128,2,32]{0,2,1:T(8,128)S(1)} all-reduce(f32[128,2,32]{0,2,1:T(8,128)S(1)} %convolution_bitcast_fusion.5), channel_id=1, replica_groups=mesh['section'=8,'tp'=16] {'tp'}, use_global_device_ids=true, to_apply=%region_2.2 | all-reduce | flops 8192 | bytes 65536 | tf_op jit(solution)/shard_map/while/body/eval_jaxpr/psum | solution.py:82
  647.3 17.7 %collective-permute-start = (bf16[128,4096]{1,0:T(8,128)(2,1)}, bf16[128,4096]{1,0:T(8,128)(2,1)S(1)}, u32[]{:S(2)}, u32[]{:S(2)}) collective-permute-start(bf16[128,4096]{1,0:T(8,128)(2,1)} %get-tuple-element.465), channel_id=1, source_target_pairs={{16,0},{32,16},{48,32},{64,48},{80,64},{96,80},{112,96},{17,1},{33... | collective-permute-start | bytes 3145736 | tf_op jit(solution)/shard_map/while/body/eval_jaxpr/ppermute | solution.py:15
  665.0 13.7 collective-permute-done
  683.4 37.6 %all-gather.3.cloned.1.call-done = bf16[128,4096]{1,0:T(8,128)(2,1)} async-done(((bf16[128,256]{1,0:T(8,128)(2,1)}), bf16[128,4096]{1,0:T(8,128)(2,1)}) %all-gather.3.cloned.1.call-update) | async-done | bytes 1048592 | tf_op jit(solution)/shard_map/while/body/eval_jaxpr/all_gather | solution.py:73
  726.7 58.4 %psum.31 = f32[128,2,32]{0,2,1:T(8,128)S(1)} all-reduce(f32[128,2,32]{0,2,1:T(8,128)S(1)} %convolution_bitcast_fusion.5), channel_id=1, replica_groups=mesh['section'=8,'tp'=16] {'tp'}, use_global_device_ids=true, to_apply=%region_2.2 | all-reduce | flops 8192 | bytes 65536 | tf_op jit(solution)/shard_map/while/body/eval_jaxpr/psum | solution.py:82
  787.3 17.7 %collective-permute-start = (bf16[128,4096]{1,0:T(8,128)(2,1)}, bf16[128,4096]{1,0:T(8,128)(2,1)S(1)}, u32[]{:S(2)}, u32[]{:S(2)}) collective-permute-start(bf16[128,4096]{1,0:T(8,128)(2,1)} %get-tuple-element.465), channel_id=1, source_target_pairs={{16,0},{32,16},{48,32},{64,48},{80,64},{96,80},{112,96},{17,1},{33... | collective-permute-start | bytes 3145736 | tf_op jit(solution)/shard_map/while/body/eval_jaxpr/ppermute | solution.py:15
  805.0 13.7 collective-permute-done
  823.4 37.6 %all-gather.3.cloned.1.call-done = bf16[128,4096]{1,0:T(8,128)(2,1)} async-done(((bf16[128,256]{1,0:T(8,128)(2,1)}), bf16[128,4096]{1,0:T(8,128)(2,1)}) %all-gather.3.cloned.1.call-update) | async-done | bytes 1048592 | tf_op jit(solution)/shard_map/while/body/eval_jaxpr/all_gather | solution.py:73
  866.7 58.4 %psum.31 = f32[128,2,32]{0,2,1:T(8,128)S(1)} all-reduce(f32[128,2,32]{0,2,1:T(8,128)S(1)} %convolution_bitcast_fusion.5), channel_id=1, replica_groups=mesh['section'=8,'tp'=16] {'tp'}, use_global_device_ids=true, to_apply=%region_2.2 | all-reduce | flops 8192 | bytes 65536 | tf_op jit(solution)/shard_map/while/body/eval_jaxpr/psum | solution.py:82
  927.4 17.7 %collective-permute-start = (bf16[128,4096]{1,0:T(8,128)(2,1)}, bf16[128,4096]{1,0:T(8,128)(2,1)S(1)}, u32[]{:S(2)}, u32[]{:S(2)}) collective-permute-start(bf16[128,4096]{1,0:T(8,128)(2,1)} %get-tuple-element.465), channel_id=1, source_target_pairs={{16,0},{32,16},{48,32},{64,48},{80,64},{96,80},{112,96},{17,1},{33... | collective-permute-start | bytes 3145736 | tf_op jit(solution)/shard_map/while/body/eval_jaxpr/ppermute | solution.py:15
  945.1 13.7 collective-permute-done
  963.4 37.6 %all-gather.3.cloned.1.call-done = bf16[128,4096]{1,0:T(8,128)(2,1)} async-done(((bf16[128,256]{1,0:T(8,128)(2,1)}), bf16[128,4096]{1,0:T(8,128)(2,1)}) %all-gather.3.cloned.1.call-update) | async-done | bytes 1048592 | tf_op jit(solution)/shard_map/while/body/eval_jaxpr/all_gather | solution.py:73
  1006.7 58.4 %psum.31 = f32[128,2,32]{0,2,1:T(8,128)S(1)} all-reduce(f32[128,2,32]{0,2,1:T(8,128)S(1)} %convolution_bitcast_fusion.5), channel_id=1, replica_groups=mesh['section'=8,'tp'=16] {'tp'}, use_global_device_ids=true, to_apply=%region_2.2 | all-reduce | flops 8192 | bytes 65536 | tf_op jit(solution)/shard_map/while/body/eval_jaxpr/psum | solution.py:82
  1067.4 17.7 %collective-permute-start = (bf16[128,4096]{1,0:T(8,128)(2,1)}, bf16[128,4096]{1,0:T(8,128)(2,1)S(1)}, u32[]{:S(2)}, u32[]{:S(2)}) collective-permute-start(bf16[128,4096]{1,0:T(8,128)(2,1)} %get-tuple-element.465), channel_id=1, source_target_pairs={{16,0},{32,16},{48,32},{64,48},{80,64},{96,80},{112,96},{17,1},{33... | collective-permute-start | bytes 3145736 | tf_op jit(solution)/shard_map/while/body/eval_jaxpr/ppermute | solution.py:15
  1085.1 13.7 collective-permute-done
  1103.5 37.6 %all-gather.3.cloned.1.call-done = bf16[128,4096]{1,0:T(8,128)(2,1)} async-done(((bf16[128,256]{1,0:T(8,128)(2,1)}), bf16[128,4096]{1,0:T(8,128)(2,1)}) %all-gather.3.cloned.1.call-update) | async-done | bytes 1048592 | tf_op jit(solution)/shard_map/while/body/eval_jaxpr/all_gather | solution.py:73
  1146.8 58.4 %psum.31 = f32[128,2,32]{0,2,1:T(8,128)S(1)} all-reduce(f32[128,2,32]{0,2,1:T(8,128)S(1)} %convolution_bitcast_fusion.5), channel_id=1, replica_groups=mesh['section'=8,'tp'=16] {'tp'}, use_global_device_ids=true, to_apply=%region_2.2 | all-reduce | flops 8192 | bytes 65536 | tf_op jit(solution)/shard_map/while/body/eval_jaxpr/psum | solution.py:82
  1207.4 17.7 %collective-permute-start = (bf16[128,4096]{1,0:T(8,128)(2,1)}, bf16[128,4096]{1,0:T(8,128)(2,1)S(1)}, u32[]{:S(2)}, u32[]{:S(2)}) collective-permute-start(bf16[128,4096]{1,0:T(8,128)(2,1)} %get-tuple-element.465), channel_id=1, source_target_pairs={{16,0},{32,16},{48,32},{64,48},{80,64},{96,80},{112,96},{17,1},{33... | collective-permute-start | bytes 3145736 | tf_op jit(solution)/shard_map/while/body/eval_jaxpr/ppermute | solution.py:15
  1225.1 13.7 collective-permute-done
  1243.5 37.6 %all-gather.3.cloned.1.call-done = bf16[128,4096]{1,0:T(8,128)(2,1)} async-done(((bf16[128,256]{1,0:T(8,128)(2,1)}), bf16[128,4096]{1,0:T(8,128)(2,1)}) %all-gather.3.cloned.1.call-update) | async-done | bytes 1048592 | tf_op jit(solution)/shard_map/while/body/eval_jaxpr/all_gather | solution.py:73
  1286.8 58.4 %psum.31 = f32[128,2,32]{0,2,1:T(8,128)S(1)} all-reduce(f32[128,2,32]{0,2,1:T(8,128)S(1)} %convolution_bitcast_fusion.5), channel_id=1, replica_groups=mesh['section'=8,'tp'=16] {'tp'}, use_global_device_ids=true, to_apply=%region_2.2 | all-reduce | flops 8192 | bytes 65536 | tf_op jit(solution)/shard_map/while/body/eval_jaxpr/psum | solution.py:82
  1347.4 17.7 %collective-permute-start = (bf16[128,4096]{1,0:T(8,128)(2,1)}, bf16[128,4096]{1,0:T(8,128)(2,1)S(1)}, u32[]{:S(2)}, u32[]{:S(2)}) collective-permute-start(bf16[128,4096]{1,0:T(8,128)(2,1)} %get-tuple-element.465), channel_id=1, source_target_pairs={{16,0},{32,16},{48,32},{64,48},{80,64},{96,80},{112,96},{17,1},{33... | collective-permute-start | bytes 3145736 | tf_op jit(solution)/shard_map/while/body/eval_jaxpr/ppermute | solution.py:15
  1365.1 13.7 collective-permute-done
  1383.5 37.6 %all-gather.3.cloned.1.call-done = bf16[128,4096]{1,0:T(8,128)(2,1)} async-done(((bf16[128,256]{1,0:T(8,128)(2,1)}), bf16[128,4096]{1,0:T(8,128)(2,1)}) %all-gather.3.cloned.1.call-update) | async-done | bytes 1048592 | tf_op jit(solution)/shard_map/while/body/eval_jaxpr/all_gather | solution.py:73
  1426.8 58.4 %psum.31 = f32[128,2,32]{0,2,1:T(8,128)S(1)} all-reduce(f32[128,2,32]{0,2,1:T(8,128)S(1)} %convolution_bitcast_fusion.5), channel_id=1, replica_groups=mesh['section'=8,'tp'=16] {'tp'}, use_global_device_ids=true, to_apply=%region_2.2 | all-reduce | flops 8192 | bytes 65536 | tf_op jit(solution)/shard_map/while/body/eval_jaxpr/psum | solution.py:82
  1487.5 17.7 %collective-permute-start = (bf16[128,4096]{1,0:T(8,128)(2,1)}, bf16[128,4096]{1,0:T(8,128)(2,1)S(1)}, u32[]{:S(2)}, u32[]{:S(2)}) collective-permute-start(bf16[128,4096]{1,0:T(8,128)(2,1)} %get-tuple-element.465), channel_id=1, source_target_pairs={{16,0},{32,16},{48,32},{64,48},{80,64},{96,80},{112,96},{17,1},{33... | collective-permute-start | bytes 3145736 | tf_op jit(solution)/shard_map/while/body/eval_jaxpr/ppermute | solution.py:15
  1505.2 13.7 collective-permute-done
  1523.5 37.6 %all-gather.3.cloned.1.call-done = bf16[128,4096]{1,0:T(8,128)(2,1)} async-done(((bf16[128,256]{1,0:T(8,128)(2,1)}), bf16[128,4096]{1,0:T(8,128)(2,1)}) %all-gather.3.cloned.1.call-update) | async-done | bytes 1048592 | tf_op jit(solution)/shard_map/while/body/eval_jaxpr/all_gather | solution.py:73
  1566.8 58.4 %psum.31 = f32[128,2,32]{0,2,1:T(8,128)S(1)} all-reduce(f32[128,2,32]{0,2,1:T(8,128)S(1)} %convolution_bitcast_fusion.5), channel_id=1, replica_groups=mesh['section'=8,'tp'=16] {'tp'}, use_global_device_ids=true, to_apply=%region_2.2 | all-reduce | flops 8192 | bytes 65536 | tf_op jit(solution)/shard_map/while/body/eval_jaxpr/psum | solution.py:82
  1627.8 28.1 %psum.28 = f32[2,32]{1,0:T(2,128)} all-reduce(f32[2,32]{1,0:T(2,128)S(1)} %convolution_bitcast_fusion.3), channel_id=1, replica_groups=mesh['section'=8,'tp'=16] {'section'}, use_global_device_ids=true, to_apply=%region_4.5 | all-reduce | flops 64 | bytes 512 | tf_op jit(solution)/shard_map/psum | solution.py:107
  (201 shorter events, 137.2 us)
Async XLA Ops:
  6.5 1620.9 %copy-start = (bf16[2,32,2048]{2,1,0:T(8,128)(2,1)S(1)}, bf16[2,32,2048]{2,1,0:T(8,128)(2,1)}, u32[]{:S(2)}) copy-start(bf16[2,32,2048]{2,1,0:T(8,128)(2,1)} %param.13) | copy-start | bytes 786436
  6.5 90.4 %all-reduce.2.cloned.1.call-start = ((), (), s32[]{:S(2)}) async-start(), calls=%async_computation | async-start | bytes 524288 | tf_op jit(solution)/shard_map/psum | solution.py:49
  8.8 89.2 %copy-start.3 = (bf16[2,256,32]{1,2,0:T(8,128)(2,1)S(1)}, bf16[2,256,32]{1,2,0:T(8,128)(2,1)}, u32[]{:S(2)}) copy-start(bf16[2,256,32]{1,2,0:T(8,128)(2,1)} %param.12) | copy-start | bytes 98308
  8.8 89.2 %copy-start.4 = (s32[4]{0:T(128)S(1)}, s32[4]{0:T(128)}, u32[]{:S(2)}) copy-start(s32[4]{0:T(128)} %param.15) | copy-start | bytes 52
  98.0 62.9 %all-gather.3.cloned.1.call-start = ((), (), s32[]{:S(2)}) async-start(), calls=%async_computation.1 | async-start | bytes 1114112 | tf_op jit(solution)/shard_map/while/body/eval_jaxpr/all_gather | solution.py:73
  98.0 17.6 %collective-permute-start = (bf16[128,4096]{1,0:T(8,128)(2,1)}, bf16[128,4096]{1,0:T(8,128)(2,1)S(1)}, u32[]{:S(2)}, u32[]{:S(2)}) collective-permute-start(bf16[128,4096]{1,0:T(8,128)(2,1)} %get-tuple-element.465), channel_id=1, source_target_pairs={{16,0},{32,16},{48,32},{64,48},{80,64},{96,80},{112,96},{17,1},{33... | collective-permute-start | bytes 3145736 | tf_op jit(solution)/shard_map/while/body/eval_jaxpr/ppermute | solution.py:15
  120.2 46.2 %copy-start.1 = (bf16[128,256]{1,0:T(8,128)(2,1)S(1)}, bf16[128,256]{1,0:T(8,128)(2,1)}, u32[]{:S(2)}) copy-start(bf16[128,256]{1,0:T(8,128)(2,1)} %add_convert_fusion.4) | copy-start | bytes 196612 | tf_op jit(solution)/shard_map/while
  120.2 106.9 %all-gather.5.cloned.1.call-start = ((), (), s32[]{:S(2)}) async-start(), calls=%async_computation.2 | async-start | bytes 1114112 | tf_op jit(solution)/shard_map/while/body/eval_jaxpr/all_gather | solution.py:77
  227.2 73.7 %all-gather.3.cloned.1.call-start = ((), (), s32[]{:S(2)}) async-start(), calls=%async_computation.1 | async-start | bytes 1114112 | tf_op jit(solution)/shard_map/while/body/eval_jaxpr/all_gather | solution.py:73
  227.2 31.4 %collective-permute-start = (bf16[128,4096]{1,0:T(8,128)(2,1)}, bf16[128,4096]{1,0:T(8,128)(2,1)S(1)}, u32[]{:S(2)}, u32[]{:S(2)}) collective-permute-start(bf16[128,4096]{1,0:T(8,128)(2,1)} %get-tuple-element.465), channel_id=1, source_target_pairs={{16,0},{32,16},{48,32},{64,48},{80,64},{96,80},{112,96},{17,1},{33... | collective-permute-start | bytes 3145736 | tf_op jit(solution)/shard_map/while/body/eval_jaxpr/ppermute | solution.py:15
  263.2 43.2 %copy-start.1 = (bf16[128,256]{1,0:T(8,128)(2,1)S(1)}, bf16[128,256]{1,0:T(8,128)(2,1)}, u32[]{:S(2)}) copy-start(bf16[128,256]{1,0:T(8,128)(2,1)} %add_convert_fusion.4) | copy-start | bytes 196612 | tf_op jit(solution)/shard_map/while
  263.3 103.9 %all-gather.5.cloned.1.call-start = ((), (), s32[]{:S(2)}) async-start(), calls=%async_computation.2 | async-start | bytes 1114112 | tf_op jit(solution)/shard_map/while/body/eval_jaxpr/all_gather | solution.py:77
  367.2 73.8 %all-gather.3.cloned.1.call-start = ((), (), s32[]{:S(2)}) async-start(), calls=%async_computation.1 | async-start | bytes 1114112 | tf_op jit(solution)/shard_map/while/body/eval_jaxpr/all_gather | solution.py:73
  367.3 31.4 %collective-permute-start = (bf16[128,4096]{1,0:T(8,128)(2,1)}, bf16[128,4096]{1,0:T(8,128)(2,1)S(1)}, u32[]{:S(2)}, u32[]{:S(2)}) collective-permute-start(bf16[128,4096]{1,0:T(8,128)(2,1)} %get-tuple-element.465), channel_id=1, source_target_pairs={{16,0},{32,16},{48,32},{64,48},{80,64},{96,80},{112,96},{17,1},{33... | collective-permute-start | bytes 3145736 | tf_op jit(solution)/shard_map/while/body/eval_jaxpr/ppermute | solution.py:15
  403.3 43.2 %copy-start.1 = (bf16[128,256]{1,0:T(8,128)(2,1)S(1)}, bf16[128,256]{1,0:T(8,128)(2,1)}, u32[]{:S(2)}) copy-start(bf16[128,256]{1,0:T(8,128)(2,1)} %add_convert_fusion.4) | copy-start | bytes 196612 | tf_op jit(solution)/shard_map/while
  403.3 103.9 %all-gather.5.cloned.1.call-start = ((), (), s32[]{:S(2)}) async-start(), calls=%async_computation.2 | async-start | bytes 1114112 | tf_op jit(solution)/shard_map/while/body/eval_jaxpr/all_gather | solution.py:77
  507.2 73.8 %all-gather.3.cloned.1.call-start = ((), (), s32[]{:S(2)}) async-start(), calls=%async_computation.1 | async-start | bytes 1114112 | tf_op jit(solution)/shard_map/while/body/eval_jaxpr/all_gather | solution.py:73
  507.3 31.4 %collective-permute-start = (bf16[128,4096]{1,0:T(8,128)(2,1)}, bf16[128,4096]{1,0:T(8,128)(2,1)S(1)}, u32[]{:S(2)}, u32[]{:S(2)}) collective-permute-start(bf16[128,4096]{1,0:T(8,128)(2,1)} %get-tuple-element.465), channel_id=1, source_target_pairs={{16,0},{32,16},{48,32},{64,48},{80,64},{96,80},{112,96},{17,1},{33... | collective-permute-start | bytes 3145736 | tf_op jit(solution)/shard_map/while/body/eval_jaxpr/ppermute | solution.py:15
  543.3 43.2 %copy-start.1 = (bf16[128,256]{1,0:T(8,128)(2,1)S(1)}, bf16[128,256]{1,0:T(8,128)(2,1)}, u32[]{:S(2)}) copy-start(bf16[128,256]{1,0:T(8,128)(2,1)} %add_convert_fusion.4) | copy-start | bytes 196612 | tf_op jit(solution)/shard_map/while
  543.3 103.9 %all-gather.5.cloned.1.call-start = ((), (), s32[]{:S(2)}) async-start(), calls=%async_computation.2 | async-start | bytes 1114112 | tf_op jit(solution)/shard_map/while/body/eval_jaxpr/all_gather | solution.py:77
  647.3 73.8 %all-gather.3.cloned.1.call-start = ((), (), s32[]{:S(2)}) async-start(), calls=%async_computation.1 | async-start | bytes 1114112 | tf_op jit(solution)/shard_map/while/body/eval_jaxpr/all_gather | solution.py:73
  647.3 31.4 %collective-permute-start = (bf16[128,4096]{1,0:T(8,128)(2,1)}, bf16[128,4096]{1,0:T(8,128)(2,1)S(1)}, u32[]{:S(2)}, u32[]{:S(2)}) collective-permute-start(bf16[128,4096]{1,0:T(8,128)(2,1)} %get-tuple-element.465), channel_id=1, source_target_pairs={{16,0},{32,16},{48,32},{64,48},{80,64},{96,80},{112,96},{17,1},{33... | collective-permute-start | bytes 3145736 | tf_op jit(solution)/shard_map/while/body/eval_jaxpr/ppermute | solution.py:15
  683.3 43.2 %copy-start.1 = (bf16[128,256]{1,0:T(8,128)(2,1)S(1)}, bf16[128,256]{1,0:T(8,128)(2,1)}, u32[]{:S(2)}) copy-start(bf16[128,256]{1,0:T(8,128)(2,1)} %add_convert_fusion.4) | copy-start | bytes 196612 | tf_op jit(solution)/shard_map/while
  683.3 103.9 %all-gather.5.cloned.1.call-start = ((), (), s32[]{:S(2)}) async-start(), calls=%async_computation.2 | async-start | bytes 1114112 | tf_op jit(solution)/shard_map/while/body/eval_jaxpr/all_gather | solution.py:77
  787.3 73.8 %all-gather.3.cloned.1.call-start = ((), (), s32[]{:S(2)}) async-start(), calls=%async_computation.1 | async-start | bytes 1114112 | tf_op jit(solution)/shard_map/while/body/eval_jaxpr/all_gather | solution.py:73
  787.3 31.4 %collective-permute-start = (bf16[128,4096]{1,0:T(8,128)(2,1)}, bf16[128,4096]{1,0:T(8,128)(2,1)S(1)}, u32[]{:S(2)}, u32[]{:S(2)}) collective-permute-start(bf16[128,4096]{1,0:T(8,128)(2,1)} %get-tuple-element.465), channel_id=1, source_target_pairs={{16,0},{32,16},{48,32},{64,48},{80,64},{96,80},{112,96},{17,1},{33... | collective-permute-start | bytes 3145736 | tf_op jit(solution)/shard_map/while/body/eval_jaxpr/ppermute | solution.py:15
  823.3 43.2 %copy-start.1 = (bf16[128,256]{1,0:T(8,128)(2,1)S(1)}, bf16[128,256]{1,0:T(8,128)(2,1)}, u32[]{:S(2)}) copy-start(bf16[128,256]{1,0:T(8,128)(2,1)} %add_convert_fusion.4) | copy-start | bytes 196612 | tf_op jit(solution)/shard_map/while
  823.4 103.9 %all-gather.5.cloned.1.call-start = ((), (), s32[]{:S(2)}) async-start(), calls=%async_computation.2 | async-start | bytes 1114112 | tf_op jit(solution)/shard_map/while/body/eval_jaxpr/all_gather | solution.py:77
  927.3 73.8 %all-gather.3.cloned.1.call-start = ((), (), s32[]{:S(2)}) async-start(), calls=%async_computation.1 | async-start | bytes 1114112 | tf_op jit(solution)/shard_map/while/body/eval_jaxpr/all_gather | solution.py:73
  927.4 31.4 %collective-permute-start = (bf16[128,4096]{1,0:T(8,128)(2,1)}, bf16[128,4096]{1,0:T(8,128)(2,1)S(1)}, u32[]{:S(2)}, u32[]{:S(2)}) collective-permute-start(bf16[128,4096]{1,0:T(8,128)(2,1)} %get-tuple-element.465), channel_id=1, source_target_pairs={{16,0},{32,16},{48,32},{64,48},{80,64},{96,80},{112,96},{17,1},{33... | collective-permute-start | bytes 3145736 | tf_op jit(solution)/shard_map/while/body/eval_jaxpr/ppermute | solution.py:15
  963.4 43.2 %copy-start.1 = (bf16[128,256]{1,0:T(8,128)(2,1)S(1)}, bf16[128,256]{1,0:T(8,128)(2,1)}, u32[]{:S(2)}) copy-start(bf16[128,256]{1,0:T(8,128)(2,1)} %add_convert_fusion.4) | copy-start | bytes 196612 | tf_op jit(solution)/shard_map/while
  963.4 103.9 %all-gather.5.cloned.1.call-start = ((), (), s32[]{:S(2)}) async-start(), calls=%async_computation.2 | async-start | bytes 1114112 | tf_op jit(solution)/shard_map/while/body/eval_jaxpr/all_gather | solution.py:77
  1067.3 73.8 %all-gather.3.cloned.1.call-start = ((), (), s32[]{:S(2)}) async-start(), calls=%async_computation.1 | async-start | bytes 1114112 | tf_op jit(solution)/shard_map/while/body/eval_jaxpr/all_gather | solution.py:73
  1067.4 31.4 %collective-permute-start = (bf16[128,4096]{1,0:T(8,128)(2,1)}, bf16[128,4096]{1,0:T(8,128)(2,1)S(1)}, u32[]{:S(2)}, u32[]{:S(2)}) collective-permute-start(bf16[128,4096]{1,0:T(8,128)(2,1)} %get-tuple-element.465), channel_id=1, source_target_pairs={{16,0},{32,16},{48,32},{64,48},{80,64},{96,80},{112,96},{17,1},{33... | collective-permute-start | bytes 3145736 | tf_op jit(solution)/shard_map/while/body/eval_jaxpr/ppermute | solution.py:15
  1103.4 43.2 %copy-start.1 = (bf16[128,256]{1,0:T(8,128)(2,1)S(1)}, bf16[128,256]{1,0:T(8,128)(2,1)}, u32[]{:S(2)}) copy-start(bf16[128,256]{1,0:T(8,128)(2,1)} %add_convert_fusion.4) | copy-start | bytes 196612 | tf_op jit(solution)/shard_map/while
  1103.4 103.9 %all-gather.5.cloned.1.call-start = ((), (), s32[]{:S(2)}) async-start(), calls=%async_computation.2 | async-start | bytes 1114112 | tf_op jit(solution)/shard_map/while/body/eval_jaxpr/all_gather | solution.py:77
  1207.4 73.8 %all-gather.3.cloned.1.call-start = ((), (), s32[]{:S(2)}) async-start(), calls=%async_computation.1 | async-start | bytes 1114112 | tf_op jit(solution)/shard_map/while/body/eval_jaxpr/all_gather | solution.py:73
  1207.4 31.4 %collective-permute-start = (bf16[128,4096]{1,0:T(8,128)(2,1)}, bf16[128,4096]{1,0:T(8,128)(2,1)S(1)}, u32[]{:S(2)}, u32[]{:S(2)}) collective-permute-start(bf16[128,4096]{1,0:T(8,128)(2,1)} %get-tuple-element.465), channel_id=1, source_target_pairs={{16,0},{32,16},{48,32},{64,48},{80,64},{96,80},{112,96},{17,1},{33... | collective-permute-start | bytes 3145736 | tf_op jit(solution)/shard_map/while/body/eval_jaxpr/ppermute | solution.py:15
  1243.4 43.2 %copy-start.1 = (bf16[128,256]{1,0:T(8,128)(2,1)S(1)}, bf16[128,256]{1,0:T(8,128)(2,1)}, u32[]{:S(2)}) copy-start(bf16[128,256]{1,0:T(8,128)(2,1)} %add_convert_fusion.4) | copy-start | bytes 196612 | tf_op jit(solution)/shard_map/while
  1243.4 103.9 %all-gather.5.cloned.1.call-start = ((), (), s32[]{:S(2)}) async-start(), calls=%async_computation.2 | async-start | bytes 1114112 | tf_op jit(solution)/shard_map/while/body/eval_jaxpr/all_gather | solution.py:77
  1347.4 73.8 %all-gather.3.cloned.1.call-start = ((), (), s32[]{:S(2)}) async-start(), calls=%async_computation.1 | async-start | bytes 1114112 | tf_op jit(solution)/shard_map/while/body/eval_jaxpr/all_gather | solution.py:73
  1347.4 31.4 %collective-permute-start = (bf16[128,4096]{1,0:T(8,128)(2,1)}, bf16[128,4096]{1,0:T(8,128)(2,1)S(1)}, u32[]{:S(2)}, u32[]{:S(2)}) collective-permute-start(bf16[128,4096]{1,0:T(8,128)(2,1)} %get-tuple-element.465), channel_id=1, source_target_pairs={{16,0},{32,16},{48,32},{64,48},{80,64},{96,80},{112,96},{17,1},{33... | collective-permute-start | bytes 3145736 | tf_op jit(solution)/shard_map/while/body/eval_jaxpr/ppermute | solution.py:15
  1383.4 43.2 %copy-start.1 = (bf16[128,256]{1,0:T(8,128)(2,1)S(1)}, bf16[128,256]{1,0:T(8,128)(2,1)}, u32[]{:S(2)}) copy-start(bf16[128,256]{1,0:T(8,128)(2,1)} %add_convert_fusion.4) | copy-start | bytes 196612 | tf_op jit(solution)/shard_map/while
  1383.5 103.9 %all-gather.5.cloned.1.call-start = ((), (), s32[]{:S(2)}) async-start(), calls=%async_computation.2 | async-start | bytes 1114112 | tf_op jit(solution)/shard_map/while/body/eval_jaxpr/all_gather | solution.py:77
  1487.4 73.8 %all-gather.3.cloned.1.call-start = ((), (), s32[]{:S(2)}) async-start(), calls=%async_computation.1 | async-start | bytes 1114112 | tf_op jit(solution)/shard_map/while/body/eval_jaxpr/all_gather | solution.py:73
  1487.5 31.4 %collective-permute-start = (bf16[128,4096]{1,0:T(8,128)(2,1)}, bf16[128,4096]{1,0:T(8,128)(2,1)S(1)}, u32[]{:S(2)}, u32[]{:S(2)}) collective-permute-start(bf16[128,4096]{1,0:T(8,128)(2,1)} %get-tuple-element.465), channel_id=1, source_target_pairs={{16,0},{32,16},{48,32},{64,48},{80,64},{96,80},{112,96},{17,1},{33... | collective-permute-start | bytes 3145736 | tf_op jit(solution)/shard_map/while/body/eval_jaxpr/ppermute | solution.py:15
  1523.5 43.2 %copy-start.1 = (bf16[128,256]{1,0:T(8,128)(2,1)S(1)}, bf16[128,256]{1,0:T(8,128)(2,1)}, u32[]{:S(2)}) copy-start(bf16[128,256]{1,0:T(8,128)(2,1)} %add_convert_fusion.4) | copy-start | bytes 196612 | tf_op jit(solution)/shard_map/while
  1523.5 103.9 %all-gather.5.cloned.1.call-start = ((), (), s32[]{:S(2)}) async-start(), calls=%async_computation.2 | async-start | bytes 1114112 | tf_op jit(solution)/shard_map/while/body/eval_jaxpr/all_gather | solution.py:77
  (1 other events, 2.3 us)
Sparse Core Ops, SparseCore 0:
  10.5 86.3 all-reduce.1
  120.3 40.5 all-gather.2
  164.4 42.9 all-gather.4
  263.4 37.5 all-gather.2
  304.4 42.9 all-gather.4
  403.4 37.5 all-gather.2
  444.4 42.9 all-gather.4
  543.4 37.5 all-gather.2
  584.5 42.9 all-gather.4
  683.4 37.5 all-gather.2
  724.5 42.9 all-gather.4
  823.5 37.5 all-gather.2
  864.5 42.9 all-gather.4
  963.5 37.5 all-gather.2
  1004.5 42.9 all-gather.4
  1103.5 37.5 all-gather.2
  1144.6 42.9 all-gather.4
  1243.5 37.5 all-gather.2
  1284.6 42.9 all-gather.4
  1383.6 37.5 all-gather.2
  1424.6 42.9 all-gather.4
  1523.6 37.5 all-gather.2
  1564.6 42.9 all-gather.4
where the time goes:
time: 1660 us
  blocking collectives  671 us (40%)
  waiting for transfers between devices  657 us (40%)
  starting transfers between devices  182 us (11%)
  matrix products  95 us (6%)
  other arithmetic  26.3 us (2%)
  local copies, waits for them, and re-layouts  17.8 us (1%)
    psum x11, blocking collectives, tick(): lax.psum(partial_out.reshape(block_rows, -1), 'tp')  643 us
    all_gather x11, waiting for transfers between devices, tick(): lax.all_gather(middle_own, 'tp', axis=1, tiled=True)  417 us
    ppermute x11, starting transfers between devices, from_behind(): return lax.ppermute(value, axis, pairs)  181 us
    ppermute x11, waiting for transfers between devices, from_behind(): return lax.ppermute(value, axis, pairs)  151 us
    psum x1, waiting for transfers between devices, shards(): lax.psum(partial_in.reshape(total_tokens, -1), 'tp')  87.7 us
    dot_general x11, matrix products, contract_columns(): lax.dot_general(portion, matrix, (((1,), (1,)), ((), ())), preferred_elem...  36.4 us
    dot_general x11, matrix products, tick(): lax.dot_general(upper_full, weights[1], (((1,), (1,)), ((), ())), preferr...  33.7 us
  transfers between devices with their start and end apart: 34, of which 23 were waited for; matrix products, arithmetic and copies ran while one was open for 3% of the time, Pallas kernels for 0%

commit v1 on v0

--- a/solution.py
+++ b/solution.py
@@ -70,7 +70,30 @@
         middle_own = (upper_own.astype(jnp.float32) + slope_block[1] * upper_branch).astype(
             jnp.bfloat16
         )
-        lower_branch = fold_lower(lax.all_gather(middle_own, "tp", axis=1, tiled=True))
+
+        def group_side_on_mesh(sample):
+            built = lax.psum(1, axis_name="tp")
+            n_now = lax.axis_index("tp")
+            carry, work_now, z2 = (built, n_now, sample.shape[1])
+            store = [at * carry if k == 1 else at for k, at in enumerate(sample.shape)]
+            heard = jnp.zeros(store, sample.dtype)
+            v1 = lax.dynamic_update_slice_in_dim(heard, sample, work_now * z2, axis=1)
+            big = low = sample
+            for p in range(1, carry // 2 + 1):
+                big = lax.ppermute(
+                    big, axis_name="tp", perm=[(k, (k + 1) % carry) for k in range(carry)]
+                )
+                v1 = lax.dynamic_update_slice_in_dim(v1, big, (work_now - p) % carry * z2, axis=1)
+                if 2 * p < carry:
+                    low = lax.ppermute(
+                        low, axis_name="tp", perm=[(k, (k - 1) % carry) for k in range(carry)]
+                    )
+                    v1 = lax.dynamic_update_slice_in_dim(
+                        v1, low, (work_now + p) % carry * z2, axis=1
+                    )
+            return v1
+
+        lower_branch = fold_lower(group_side_on_mesh(middle_own))
         lower_own = (middle_own.astype(jnp.float32) + slope_block[0] * lower_branch).astype(
             jnp.bfloat16
         )

time: 1660 us -> 1870 us (1.13)
  starting transfers between devices: 182 us -> 370 us
  waiting for transfers between devices: 657 us -> 687 us
  blocking collectives: 671 us -> 648 us
    all_gather x11 -> x0, waiting for transfers between devices: 417 us -> none  [tick(): lax.all_gather(middle_own, 'tp', axis=1, tiled=True)]
    ppermute x0 -> x165, starting transfers between devices: none -> 334 us  [the longest x77 319 us: group_side_on_mesh(): lax.ppermute(low, axis_name='tp', perm=[(k, (k - 1) % carry) for k in ran...]
    ppermute x0 -> x165, waiting for transfers between devices: none -> 244 us  [the longest x88 152 us: group_side_on_mesh(): lax.ppermute(big, axis_name='tp', perm=[(k, (k + 1) % carry) for k in ran...]
    ppermute x11, waiting for transfers between devices: 151 us -> 355 us  [from_behind(): return lax.ppermute(value, axis, pairs)]
    ppermute x11, starting transfers between devices: 181 us -> 35.7 us  [from_behind(): return lax.ppermute(value, axis, pairs)]
    psum x11, blocking collectives: 643 us -> 614 us  [tick(): lax.psum(partial_out.reshape(block_rows, -1), 'tp')]
  transfers between devices with their start and end apart: 34 -> 188, of which waited for: 23 -> 127; matrix products, arithmetic and copies ran while one was open for 3% -> 3% of each run, Pallas kernels for 0% -> 0%
where the time goes in v1:
time: 1870 us
  waiting for transfers between devices  687 us (37%)
  blocking collectives  648 us (35%)
  starting transfers between devices  370 us (20%)
  matrix products  85 us (5%)
  local copies, waits for them, and re-layouts  35.6 us (2%)
  other arithmetic  28.4 us (2%)
    psum x11, blocking collectives, tick(): lax.psum(partial_out.reshape(block_rows, -1), 'tp')  614 us
    ppermute x11, waiting for transfers between devices, from_behind(): return lax.ppermute(value, axis, pairs)  355 us
    ppermute x77, starting transfers between devices, group_side_on_mesh(): lax.ppermute(low, axis_name='tp', perm=[(k, (k - 1) % carry) for k in ran...  319 us
    ppermute x88, waiting for transfers between devices, group_side_on_mesh(): lax.ppermute(big, axis_name='tp', perm=[(k, (k + 1) % carry) for k in ran...  152 us
    ppermute x77, waiting for transfers between devices, group_side_on_mesh(): lax.ppermute(low, axis_name='tp', perm=[(k, (k - 1) % carry) for k in ran...  91.1 us
    psum x1, waiting for transfers between devices, shards(): lax.psum(partial_in.reshape(total_tokens, -1), 'tp')  87.7 us
  transfers between devices with their start and end apart: 188, of which 127 were waited for; matrix products, arithmetic and copies ran while one was open for 3% of the time, Pallas kernels for 0%

profile of v1, /device:TPU:1, one launch (start us, length us, event | category | flops | bytes accessed | tf_op | source)
XLA Modules:
  0.0 1869.8 jit_solution(1526520680369008243)
XLA Ops:
  9.2 87.7 %all-reduce.2.cloned.1.call-done = f32[512,2,64]{0,2,1:T(8,128)} async-done(((f32[512,2,64]{0,2,1:T(8,128)}), f32[512,2,64]{0,2,1:T(8,128)}) %all-reduce.2.cloned.1.call-update) | async-done | bytes 262160 | tf_op jit(solution)/shard_map/psum | solution.py:49
  98.0 1730.7 %while.18 = (s32[]{:T(128)}, bf16[128,4096]{1,0:T(8,128)(2,1)}, f32[2,2,2048]{2,1,0:T(2,128)}, pred[]{:T(512)}, s32[]{:T(128)}, /*index=5*/bf16[512,4096]{1,0:T(...) while((s32[]{:T(128)}, bf16[128,4096]{1,0:T(8,128)(2,1)}, ...), condition=%wide.region_3.4_spmd.clone, body=%wide.region_1.3_spmd.clone.sunk | while | flops 555048960 | bytes 46567168 | solution.py:124
  101.9 13.7 collective-permute-done
  162.0 6.4 collective-permute-done.13
  168.4 6.4 collective-permute-done.15
  181.1 56.2 %psum.32 = f32[128,2,32]{0,2,1:T(8,128)S(1)} all-reduce(f32[128,2,32]{0,2,1:T(8,128)S(1)} %convolution_bitcast_fusion.5), channel_id=1, replica_groups=mesh['section'=8,'tp'=16] {'tp'}, use_global_device_ids=true, to_apply=%region_2.2 | all-reduce | flops 8192 | bytes 65536 | tf_op jit(solution)/shard_map/while/body/eval_jaxpr/psum | solution.py:105
  240.1 13.4 collective-permute-start
  253.5 24.0 %collective-permute-done = bf16[128,4096]{1,0:T(8,128)(2,1)S(1)} collective-permute-done((bf16[128,4096]{1,0:T(8,128)(2,1)}, bf16[128,4096]{1,0:T(8,128)(2,1)S(1)}, u32[]{:S(2)}, u32[]{:S(2)}) %collective-permute-start) | collective-permute-done | bytes 1048608 | tf_op jit(solution)/shard_map/while/body/eval_jaxpr/ppermute | solution.py:15
  321.3 6.4 collective-permute-done.13
  327.7 6.4 collective-permute-done.15
  340.4 56.1 %psum.32 = f32[128,2,32]{0,2,1:T(8,128)S(1)} all-reduce(f32[128,2,32]{0,2,1:T(8,128)S(1)} %convolution_bitcast_fusion.5), channel_id=1, replica_groups=mesh['section'=8,'tp'=16] {'tp'}, use_global_device_ids=true, to_apply=%region_2.2 | all-reduce | flops 8192 | bytes 65536 | tf_op jit(solution)/shard_map/while/body/eval_jaxpr/psum | solution.py:105
  402.5 34.0 %collective-permute-done = bf16[128,4096]{1,0:T(8,128)(2,1)S(1)} collective-permute-done((bf16[128,4096]{1,0:T(8,128)(2,1)}, bf16[128,4096]{1,0:T(8,128)(2,1)S(1)}, u32[]{:S(2)}, u32[]{:S(2)}) %collective-permute-start) | collective-permute-done | bytes 1048608 | tf_op jit(solution)/shard_map/while/body/eval_jaxpr/ppermute | solution.py:15
  480.0 6.5 collective-permute-done.13
  486.6 6.4 collective-permute-done.15
  499.3 55.8 %psum.32 = f32[128,2,32]{0,2,1:T(8,128)S(1)} all-reduce(f32[128,2,32]{0,2,1:T(8,128)S(1)} %convolution_bitcast_fusion.5), channel_id=1, replica_groups=mesh['section'=8,'tp'=16] {'tp'}, use_global_device_ids=true, to_apply=%region_2.2 | all-reduce | flops 8192 | bytes 65536 | tf_op jit(solution)/shard_map/while/body/eval_jaxpr/psum | solution.py:105
  559.8 36.0 %collective-permute-done = bf16[128,4096]{1,0:T(8,128)(2,1)S(1)} collective-permute-done((bf16[128,4096]{1,0:T(8,128)(2,1)}, bf16[128,4096]{1,0:T(8,128)(2,1)S(1)}, u32[]{:S(2)}, u32[]{:S(2)}) %collective-permute-start) | collective-permute-done | bytes 1048608 | tf_op jit(solution)/shard_map/while/body/eval_jaxpr/ppermute | solution.py:15
  639.6 6.4 collective-permute-done.13
  646.0 6.6 collective-permute-done.15
  659.0 55.8 %psum.32 = f32[128,2,32]{0,2,1:T(8,128)S(1)} all-reduce(f32[128,2,32]{0,2,1:T(8,128)S(1)} %convolution_bitcast_fusion.5), channel_id=1, replica_groups=mesh['section'=8,'tp'=16] {'tp'}, use_global_device_ids=true, to_apply=%region_2.2 | all-reduce | flops 8192 | bytes 65536 | tf_op jit(solution)/shard_map/while/body/eval_jaxpr/psum | solution.py:105
  719.5 35.0 %collective-permute-done = bf16[128,4096]{1,0:T(8,128)(2,1)S(1)} collective-permute-done((bf16[128,4096]{1,0:T(8,128)(2,1)}, bf16[128,4096]{1,0:T(8,128)(2,1)S(1)}, u32[]{:S(2)}, u32[]{:S(2)}) %collective-permute-start) | collective-permute-done | bytes 1048608 | tf_op jit(solution)/shard_map/while/body/eval_jaxpr/ppermute | solution.py:15
  798.0 6.4 collective-permute-done.13
  804.5 6.4 collective-permute-done.15
  817.2 55.7 %psum.32 = f32[128,2,32]{0,2,1:T(8,128)S(1)} all-reduce(f32[128,2,32]{0,2,1:T(8,128)S(1)} %convolution_bitcast_fusion.5), channel_id=1, replica_groups=mesh['section'=8,'tp'=16] {'tp'}, use_global_device_ids=true, to_apply=%region_2.2 | all-reduce | flops 8192 | bytes 65536 | tf_op jit(solution)/shard_map/while/body/eval_jaxpr/psum | solution.py:105
  877.6 35.8 %collective-permute-done = bf16[128,4096]{1,0:T(8,128)(2,1)S(1)} collective-permute-done((bf16[128,4096]{1,0:T(8,128)(2,1)}, bf16[128,4096]{1,0:T(8,128)(2,1)S(1)}, u32[]{:S(2)}, u32[]{:S(2)}) %collective-permute-start) | collective-permute-done | bytes 1048608 | tf_op jit(solution)/shard_map/while/body/eval_jaxpr/ppermute | solution.py:15
  957.1 6.4 collective-permute-done.13
  963.6 6.4 collective-permute-done.15
  976.3 56.2 %psum.32 = f32[128,2,32]{0,2,1:T(8,128)S(1)} all-reduce(f32[128,2,32]{0,2,1:T(8,128)S(1)} %convolution_bitcast_fusion.5), channel_id=1, replica_groups=mesh['section'=8,'tp'=16] {'tp'}, use_global_device_ids=true, to_apply=%region_2.2 | all-reduce | flops 8192 | bytes 65536 | tf_op jit(solution)/shard_map/while/body/eval_jaxpr/psum | solution.py:105
  1037.2 35.1 %collective-permute-done = bf16[128,4096]{1,0:T(8,128)(2,1)S(1)} collective-permute-done((bf16[128,4096]{1,0:T(8,128)(2,1)}, bf16[128,4096]{1,0:T(8,128)(2,1)S(1)}, u32[]{:S(2)}, u32[]{:S(2)}) %collective-permute-start) | collective-permute-done | bytes 1048608 | tf_op jit(solution)/shard_map/while/body/eval_jaxpr/ppermute | solution.py:15
  1115.7 6.4 collective-permute-done.13
  1122.1 6.4 collective-permute-done.15
  1134.8 55.7 %psum.32 = f32[128,2,32]{0,2,1:T(8,128)S(1)} all-reduce(f32[128,2,32]{0,2,1:T(8,128)S(1)} %convolution_bitcast_fusion.5), channel_id=1, replica_groups=mesh['section'=8,'tp'=16] {'tp'}, use_global_device_ids=true, to_apply=%region_2.2 | all-reduce | flops 8192 | bytes 65536 | tf_op jit(solution)/shard_map/while/body/eval_jaxpr/psum | solution.py:105
  1195.2 35.9 %collective-permute-done = bf16[128,4096]{1,0:T(8,128)(2,1)S(1)} collective-permute-done((bf16[128,4096]{1,0:T(8,128)(2,1)}, bf16[128,4096]{1,0:T(8,128)(2,1)S(1)}, u32[]{:S(2)}, u32[]{:S(2)}) %collective-permute-start) | collective-permute-done | bytes 1048608 | tf_op jit(solution)/shard_map/while/body/eval_jaxpr/ppermute | solution.py:15
  1275.0 6.4 collective-permute-done.13
  1281.4 6.7 collective-permute-done.15
  1294.4 55.9 %psum.32 = f32[128,2,32]{0,2,1:T(8,128)S(1)} all-reduce(f32[128,2,32]{0,2,1:T(8,128)S(1)} %convolution_bitcast_fusion.5), channel_id=1, replica_groups=mesh['section'=8,'tp'=16] {'tp'}, use_global_device_ids=true, to_apply=%region_2.2 | all-reduce | flops 8192 | bytes 65536 | tf_op jit(solution)/shard_map/while/body/eval_jaxpr/psum | solution.py:105
  1354.9 35.0 %collective-permute-done = bf16[128,4096]{1,0:T(8,128)(2,1)S(1)} collective-permute-done((bf16[128,4096]{1,0:T(8,128)(2,1)}, bf16[128,4096]{1,0:T(8,128)(2,1)S(1)}, u32[]{:S(2)}, u32[]{:S(2)}) %collective-permute-start) | collective-permute-done | bytes 1048608 | tf_op jit(solution)/shard_map/while/body/eval_jaxpr/ppermute | solution.py:15
  1433.5 6.4 collective-permute-done.13
  1439.9 6.4 collective-permute-done.15
  1452.7 55.6 %psum.32 = f32[128,2,32]{0,2,1:T(8,128)S(1)} all-reduce(f32[128,2,32]{0,2,1:T(8,128)S(1)} %convolution_bitcast_fusion.5), channel_id=1, replica_groups=mesh['section'=8,'tp'=16] {'tp'}, use_global_device_ids=true, to_apply=%region_2.2 | all-reduce | flops 8192 | bytes 65536 | tf_op jit(solution)/shard_map/while/body/eval_jaxpr/psum | solution.py:105
  1513.0 35.7 %collective-permute-done = bf16[128,4096]{1,0:T(8,128)(2,1)S(1)} collective-permute-done((bf16[128,4096]{1,0:T(8,128)(2,1)}, bf16[128,4096]{1,0:T(8,128)(2,1)S(1)}, u32[]{:S(2)}, u32[]{:S(2)}) %collective-permute-start) | collective-permute-done | bytes 1048608 | tf_op jit(solution)/shard_map/while/body/eval_jaxpr/ppermute | solution.py:15
  1592.6 6.4 collective-permute-done.13
  1599.0 6.7 collective-permute-done.15
  1612.0 55.9 %psum.32 = f32[128,2,32]{0,2,1:T(8,128)S(1)} all-reduce(f32[128,2,32]{0,2,1:T(8,128)S(1)} %convolution_bitcast_fusion.5), channel_id=1, replica_groups=mesh['section'=8,'tp'=16] {'tp'}, use_global_device_ids=true, to_apply=%region_2.2 | all-reduce | flops 8192 | bytes 65536 | tf_op jit(solution)/shard_map/while/body/eval_jaxpr/psum | solution.py:105
  1672.6 35.0 %collective-permute-done = bf16[128,4096]{1,0:T(8,128)(2,1)S(1)} collective-permute-done((bf16[128,4096]{1,0:T(8,128)(2,1)}, bf16[128,4096]{1,0:T(8,128)(2,1)S(1)}, u32[]{:S(2)}, u32[]{:S(2)}) %collective-permute-start) | collective-permute-done | bytes 1048608 | tf_op jit(solution)/shard_map/while/body/eval_jaxpr/ppermute | solution.py:15
  1751.1 6.4 collective-permute-done.13
  1757.6 6.4 collective-permute-done.15
  1770.3 55.6 %psum.32 = f32[128,2,32]{0,2,1:T(8,128)S(1)} all-reduce(f32[128,2,32]{0,2,1:T(8,128)S(1)} %convolution_bitcast_fusion.5), channel_id=1, replica_groups=mesh['section'=8,'tp'=16] {'tp'}, use_global_device_ids=true, to_apply=%region_2.2 | all-reduce | flops 8192 | bytes 65536 | tf_op jit(solution)/shard_map/while/body/eval_jaxpr/psum | solution.py:105
  1829.8 33.1 %psum.29 = f32[2,32]{1,0:T(2,128)} all-reduce(f32[2,32]{1,0:T(2,128)S(1)} %convolution_bitcast_fusion.3), channel_id=1, replica_groups=mesh['section'=8,'tp'=16] {'section'}, use_global_device_ids=true, to_apply=%region_4.5 | all-reduce | flops 64 | bytes 512 | tf_op jit(solution)/shard_map/psum | solution.py:130
  (738 shorter events, 608.0 us)
Async XLA Ops:
  6.5 90.4 %all-reduce.2.cloned.1.call-start = ((), (), s32[]{:S(2)}) async-start(), calls=%async_computation | async-start | bytes 524288 | tf_op jit(solution)/shard_map/psum | solution.py:49
  98.0 141.4 %all-gather.2.cloned.1.call-start = ((), (), s32[]{:S(2)}) async-start(), calls=%async_computation.1 | async-start | bytes 1114112 | tf_op jit(solution)/shard_map/while/body/eval_jaxpr/all_gather | solution.py:100
  98.0 17.6 collective-permute-start
  142.1 7.0 collective-permute-start.7
  156.8 11.6 collective-permute-start.14
  240.1 158.6 %all-gather.2.cloned.1.call-start = ((), (), s32[]{:S(2)}) async-start(), calls=%async_computation.1 | async-start | bytes 1114112 | tf_op jit(solution)/shard_map/while/body/eval_jaxpr/all_gather | solution.py:100
  240.1 37.5 %collective-permute-start = (bf16[128,4096]{1,0:T(8,128)(2,1)}, bf16[128,4096]{1,0:T(8,128)(2,1)S(1)}, u32[]{:S(2)}, u32[]{:S(2)}) collective-permute-start(bf16[128,4096]{1,0:T(8,128)(2,1)} %get-tuple-element.512), channel_id=1, source_target_pairs={{16,0},{32,16},{48,32},{64,48},{80,64},{96,80},{112,96},{17,1},{33... | collective-permute-start | bytes 3145736 | tf_op jit(solution)/shard_map/while/body/eval_jaxpr/ppermute | solution.py:15
  314.0 7.3 collective-permute-start.11
  315.3 12.4 collective-permute-start.14
  399.3 157.9 %all-gather.2.cloned.1.call-start = ((), (), s32[]{:S(2)}) async-start(), calls=%async_computation.1 | async-start | bytes 1114112 | tf_op jit(solution)/shard_map/while/body/eval_jaxpr/all_gather | solution.py:100
  399.3 37.2 %collective-permute-start = (bf16[128,4096]{1,0:T(8,128)(2,1)}, bf16[128,4096]{1,0:T(8,128)(2,1)S(1)}, u32[]{:S(2)}, u32[]{:S(2)}) collective-permute-start(bf16[128,4096]{1,0:T(8,128)(2,1)} %get-tuple-element.512), channel_id=1, source_target_pairs={{16,0},{32,16},{48,32},{64,48},{80,64},{96,80},{112,96},{17,1},{33... | collective-permute-start | bytes 3145736 | tf_op jit(solution)/shard_map/while/body/eval_jaxpr/ppermute | solution.py:15
  440.5 7.0 collective-permute-start.1
  448.5 7.0 collective-permute-start.6
  474.8 11.7 collective-permute-start.14
  557.8 159.2 %all-gather.2.cloned.1.call-start = ((), (), s32[]{:S(2)}) async-start(), calls=%async_computation.1 | async-start | bytes 1114112 | tf_op jit(solution)/shard_map/while/body/eval_jaxpr/all_gather | solution.py:100
  557.8 37.9 %collective-permute-start = (bf16[128,4096]{1,0:T(8,128)(2,1)}, bf16[128,4096]{1,0:T(8,128)(2,1)S(1)}, u32[]{:S(2)}, u32[]{:S(2)}) collective-permute-start(bf16[128,4096]{1,0:T(8,128)(2,1)} %get-tuple-element.512), channel_id=1, source_target_pairs={{16,0},{32,16},{48,32},{64,48},{80,64},{96,80},{112,96},{17,1},{33... | collective-permute-start | bytes 3145736 | tf_op jit(solution)/shard_map/while/body/eval_jaxpr/ppermute | solution.py:15
  612.8 7.4 collective-permute-start.5
  633.9 12.1 collective-permute-start.14
  717.6 157.5 %all-gather.2.cloned.1.call-start = ((), (), s32[]{:S(2)}) async-start(), calls=%async_computation.1 | async-start | bytes 1114112 | tf_op jit(solution)/shard_map/while/body/eval_jaxpr/all_gather | solution.py:100
  717.6 37.0 %collective-permute-start = (bf16[128,4096]{1,0:T(8,128)(2,1)}, bf16[128,4096]{1,0:T(8,128)(2,1)S(1)}, u32[]{:S(2)}, u32[]{:S(2)}) collective-permute-start(bf16[128,4096]{1,0:T(8,128)(2,1)} %get-tuple-element.512), channel_id=1, source_target_pairs={{16,0},{32,16},{48,32},{64,48},{80,64},{96,80},{112,96},{17,1},{33... | collective-permute-start | bytes 3145736 | tf_op jit(solution)/shard_map/while/body/eval_jaxpr/ppermute | solution.py:15
  765.2 7.0 collective-permute-start.3
  792.5 11.9 collective-permute-start.14
  875.7 159.0 %all-gather.2.cloned.1.call-start = ((), (), s32[]{:S(2)}) async-start(), calls=%async_computation.1 | async-start | bytes 1114112 | tf_op jit(solution)/shard_map/while/body/eval_jaxpr/all_gather | solution.py:100
  875.7 37.7 %collective-permute-start = (bf16[128,4096]{1,0:T(8,128)(2,1)}, bf16[128,4096]{1,0:T(8,128)(2,1)S(1)}, u32[]{:S(2)}, u32[]{:S(2)}) collective-permute-start(bf16[128,4096]{1,0:T(8,128)(2,1)} %get-tuple-element.512), channel_id=1, source_target_pairs={{16,0},{32,16},{48,32},{64,48},{80,64},{96,80},{112,96},{17,1},{33... | collective-permute-start | bytes 3145736 | tf_op jit(solution)/shard_map/while/body/eval_jaxpr/ppermute | solution.py:15
  925.4 7.0 collective-permute-start.6
  930.5 7.3 collective-permute-start.5
  952.0 11.6 collective-permute-start.14
  1035.2 157.5 %all-gather.2.cloned.1.call-start = ((), (), s32[]{:S(2)}) async-start(), calls=%async_computation.1 | async-start | bytes 1114112 | tf_op jit(solution)/shard_map/while/body/eval_jaxpr/all_gather | solution.py:100
  1035.2 37.0 %collective-permute-start = (bf16[128,4096]{1,0:T(8,128)(2,1)}, bf16[128,4096]{1,0:T(8,128)(2,1)S(1)}, u32[]{:S(2)}, u32[]{:S(2)}) collective-permute-start(bf16[128,4096]{1,0:T(8,128)(2,1)} %get-tuple-element.512), channel_id=1, source_target_pairs={{16,0},{32,16},{48,32},{64,48},{80,64},{96,80},{112,96},{17,1},{33... | collective-permute-start | bytes 3145736 | tf_op jit(solution)/shard_map/while/body/eval_jaxpr/ppermute | solution.py:15
  1082.9 6.9 collective-permute-start.3
  1110.5 11.6 collective-permute-start.14
  1193.3 159.1 %all-gather.2.cloned.1.call-start = ((), (), s32[]{:S(2)}) async-start(), calls=%async_computation.1 | async-start | bytes 1114112 | tf_op jit(solution)/shard_map/while/body/eval_jaxpr/all_gather | solution.py:100
  1193.3 37.8 %collective-permute-start = (bf16[128,4096]{1,0:T(8,128)(2,1)}, bf16[128,4096]{1,0:T(8,128)(2,1)S(1)}, u32[]{:S(2)}, u32[]{:S(2)}) collective-permute-start(bf16[128,4096]{1,0:T(8,128)(2,1)} %get-tuple-element.512), channel_id=1, source_target_pairs={{16,0},{32,16},{48,32},{64,48},{80,64},{96,80},{112,96},{17,1},{33... | collective-permute-start | bytes 3145736 | tf_op jit(solution)/shard_map/while/body/eval_jaxpr/ppermute | solution.py:15
  1248.2 7.4 collective-permute-start.5
  1269.5 11.9 collective-permute-start.14
  1353.0 157.5 %all-gather.2.cloned.1.call-start = ((), (), s32[]{:S(2)}) async-start(), calls=%async_computation.1 | async-start | bytes 1114112 | tf_op jit(solution)/shard_map/while/body/eval_jaxpr/all_gather | solution.py:100
  1353.0 36.9 %collective-permute-start = (bf16[128,4096]{1,0:T(8,128)(2,1)}, bf16[128,4096]{1,0:T(8,128)(2,1)S(1)}, u32[]{:S(2)}, u32[]{:S(2)}) collective-permute-start(bf16[128,4096]{1,0:T(8,128)(2,1)} %get-tuple-element.512), channel_id=1, source_target_pairs={{16,0},{32,16},{48,32},{64,48},{80,64},{96,80},{112,96},{17,1},{33... | collective-permute-start | bytes 3145736 | tf_op jit(solution)/shard_map/while/body/eval_jaxpr/ppermute | solution.py:15
  1400.6 7.1 collective-permute-start.3
  1427.9 12.0 collective-permute-start.14
  1511.1 159.0 %all-gather.2.cloned.1.call-start = ((), (), s32[]{:S(2)}) async-start(), calls=%async_computation.1 | async-start | bytes 1114112 | tf_op jit(solution)/shard_map/while/body/eval_jaxpr/all_gather | solution.py:100
  1511.1 37.7 %collective-permute-start = (bf16[128,4096]{1,0:T(8,128)(2,1)}, bf16[128,4096]{1,0:T(8,128)(2,1)S(1)}, u32[]{:S(2)}, u32[]{:S(2)}) collective-permute-start(bf16[128,4096]{1,0:T(8,128)(2,1)} %get-tuple-element.512), channel_id=1, source_target_pairs={{16,0},{32,16},{48,32},{64,48},{80,64},{96,80},{112,96},{17,1},{33... | collective-permute-start | bytes 3145736 | tf_op jit(solution)/shard_map/while/body/eval_jaxpr/ppermute | solution.py:15
  1560.8 7.0 collective-permute-start.6
  1565.9 7.3 collective-permute-start.5
  1587.4 11.6 collective-permute-start.14
  1670.6 157.5 %all-gather.2.cloned.1.call-start = ((), (), s32[]{:S(2)}) async-start(), calls=%async_computation.1 | async-start | bytes 1114112 | tf_op jit(solution)/shard_map/while/body/eval_jaxpr/all_gather | solution.py:100
  1670.6 36.9 %collective-permute-start = (bf16[128,4096]{1,0:T(8,128)(2,1)}, bf16[128,4096]{1,0:T(8,128)(2,1)S(1)}, u32[]{:S(2)}, u32[]{:S(2)}) collective-permute-start(bf16[128,4096]{1,0:T(8,128)(2,1)} %get-tuple-element.512), channel_id=1, source_target_pairs={{16,0},{32,16},{48,32},{64,48},{80,64},{96,80},{112,96},{17,1},{33... | collective-permute-start | bytes 3145736 | tf_op jit(solution)/shard_map/while/body/eval_jaxpr/ppermute | solution.py:15
  1718.3 7.1 collective-permute-start.3
  1745.6 12.0 collective-permute-start.14
  (187 other events, 3516.8 us)
Sparse Core Ops, SparseCore 0:
  10.5 86.3 all-reduce.1
  178.0 46.2 all-gather.1
  337.3 46.3 all-gather.1
  496.2 46.3 all-gather.1
  655.9 45.4 all-gather.1
  814.1 46.0 all-gather.1
  973.2 45.7 all-gather.1
  1131.7 46.0 all-gather.1
  1291.3 45.2 all-gather.1
  1449.6 45.8 all-gather.1
  1608.9 45.2 all-gather.1
  1767.2 45.8 all-gather.1
